TPU v7x, 256 devices: a whole 4x4x8 slice. The times are simulated.
256 devices in a mesh: buf: 32 (over x, y, core), lat: 8 (over z).
Axes of the slice: x: 4, y: 4, z: 8, core: 2. Of those that a mesh axis runs over, the one named last changes fastest.
Arguments:
- buffer: bfloat16 [8192, 4096], P('buf'), may hold values from -6 to 6
- sample_rows: int32 [8192], P('lat'), may hold values from 0 to 8191, as said below
- window: bfloat16 [24576, 4096], P('buf'), may hold values from -6 to 6
- enc_scale: float32 [8192], P('lat'), may hold values from 0.5 to 2
- dec_bias: float32 [4096], replicated, may hold values from -3 to 3
Outputs:
- recon: bfloat16 [24576, 4096], P('buf', 'lat')
Inputs may be any that keep to these rules, and one draw needn't show every extreme that they name: `sample_rows`: entry k names the buffer row sampled for reseeded latent k; shard s of the buffer holds rows s * 256 to (s + 1) * 256 - 1. In each aligned block of 32 entries at most 2 name rows of one shard, and in every block some shard gives exactly 2. In each owner's 1024 entries at most 64 name rows of one shard, and some shard gives exactly 64.
All inputs are finite; a program needn't handle non-finite values.
Results may differ from a plain program's by a relative error of at most 0.018.
Values may be sent and summed in bfloat16 or wider, within the bound.
A program may use at most 128 MiB of HBM per device.

v0:
```python
import jax
import jax.numpy as jnp
from jax import lax
from jax.sharding import PartitionSpec as P


def unit_rows(picked_rows):
    values = picked_rows.astype(jnp.float32)
    squares = jnp.sum(values * values, axis=1, keepdims=True)
    return (values * lax.rsqrt(squares + 1e-06)).astype(jnp.bfloat16)


def encode_block(centered, unit_block, scale_block):
    scores = lax.dot_general(
        centered, unit_block, (((1,), (1,)), ((), ())), preferred_element_type=jnp.float32
    )
    return jnp.maximum(scores * scale_block[None, :], 0.0).astype(jnp.bfloat16)


def pick_units(buffer, pick_index):
    picked = jnp.take(buffer, jnp.maximum(pick_index, 0), axis=0)
    picked = jnp.where((pick_index >= 0)[:, None], picked, jnp.zeros_like(picked))
    return unit_rows(picked)


def on_device(buffer, sample_rows, window, enc_scale, dec_bias):
    shard_count = lax.axis_size("buf")
    shard_index = lax.axis_index("buf")
    owner_count = sample_rows.shape[0]
    slot_count = owner_count // shard_count
    shard_rows = buffer.shape[0]
    capacity = 2 + (slot_count - 1) // shard_count
    source = sample_rows // shard_rows
    offset = sample_rows - source * shard_rows
    centered = (window.astype(jnp.float32) - dec_bias[None, :]).astype(jnp.bfloat16)
    positions = jnp.arange(owner_count, dtype=jnp.int32)
    own_capacity = shard_count * capacity
    matching = source[:, None] == source[None, :]
    earlier = positions[:, None] < positions[None, :]
    owner_rank = jnp.sum((matching & earlier).astype(jnp.int32), axis=0)
    room_iota = jnp.arange(own_capacity, dtype=jnp.int32)
    chosen = (source == shard_index)[:, None] & (owner_rank[:, None] == room_iota[None, :])
    pick_index = jnp.sum(jnp.where(chosen, offset[:, None] + 1, 0), axis=0) - 1
    packed = pick_units(buffer, pick_index)
    collected = lax.all_gather(packed, "buf", axis=0, tiled=True)
    all_units = jnp.take(collected, source * own_capacity + owner_rank, axis=0)
    active_all = encode_block(centered, all_units, enc_scale)
    partial_value = jnp.dot(active_all, all_units, preferred_element_type=jnp.float32)
    rounded = partial_value.astype(jnp.bfloat16).astype(jnp.float32)
    summed = lax.psum_scatter(
        rounded.astype(jnp.bfloat16), "lat", scatter_dimension=1, tiled=True
    ).astype(jnp.float32)
    feature_count = summed.shape[1]
    bias_part = lax.dynamic_slice_in_dim(
        dec_bias, lax.axis_index("lat") * feature_count, feature_count
    )
    return (summed + bias_part[None, :]).astype(jnp.bfloat16)


def solution(mesh):
    in_specs = (P("buf", None), P("lat"), P("buf", None), P("lat"), P())
    out_specs = P("buf", "lat")
    return jax.shard_map(
        on_device, mesh=mesh, in_specs=in_specs, out_specs=out_specs, check_vma=False
    )
```

profile of v0, /device:TPU:2, one launch (start us, length us, event | category | flops | bytes accessed | tf_op | source)
XLA Modules:
  0.0 219.6 jit_solution(11854953599494018754)
XLA Ops:
  6.5 0.0 copy-start
  6.5 0.0 all-gather.2.cloned.1.call-start
  6.5 0.8 add_select_fusion
  7.4 0.4 convert_reduce_fusion
  7.8 0.7 broadcast_clamp_fusion
  8.5 0.7 compare_and_fusion
  9.2 0.2 select_reduce_fusion
  9.4 0.0 copy-done
  9.4 0.9 gather_fusion
  10.3 0.3 fusion.3
  10.6 1.0 fusion.4
  11.7 0.0 all-gather.2.cloned.1.call-update
  11.7 0.0 reduce-scatter.2.cloned.1.call-start
  11.7 80.5 %all-gather.2.cloned.1.call-done = bf16[2048,4096]{1,0:T(8,128)(2,1)} async-done(((bf16[64,4096]{1,0:T(8,128)(2,1)}), bf16[2048,4096]{1,0:T(8,128)(2,1)}) %all-gather.2.cloned.1.call-update) | async-done | bytes 16777232 | tf_op jit(solution)/shard_map/all_gather | solution.py:45
  92.3 23.0 %gather_fusion.1 = bf16[1024,4096]{1,0:T(8,128)(2,1)} fusion(bf16[2048,4096]{1,0:T(8,128)(2,1)} %all-gather.2.cloned.1.call-done, s32[1024]{0:T(1024)S(1)} %get-tuple-element.7), kind=kCustom, calls=%fused_computation.1 | custom fusion | bytes 16781312 | tf_op jit(solution)/shard_map/jit(_take)/gather | solution.py:46
  115.3 0.0 copy-done.2
  115.3 0.0 copy-done.3
  115.3 11.6 %maximum_convert_fusion = bf16[768,1024]{1,0:T(8,128)(2,1)S(1)} fusion(bf16[1024,4096]{1,0:T(8,128)(2,1)} %gather_fusion.1, pred[1024]{0:T(1024)(128)(4,1)S(1)} %get-tuple-element.5, bf16[768,4096]{1,0:T(8,128)(2,1)} %param.7, f32[4096]{0:T(1024)S(1)} %copy-done.2, f32[1024]{0:T(1024)S(1)} %copy-done.3), kind=kOutput, calls=%fused_computation.10 | convolution fusion | flops 6458441728 | bytes 16274432 | tf_op jit(solution)/shard_map/dot_general | solution.py:14
  127.0 0.0 copy-done.1
  127.0 8.8 %convolution_convert_fusion = bf16[768,4096]{1,0:T(8,128)(2,1)} fusion(bf16[768,1024]{1,0:T(8,128)(2,1)S(1)} %maximum_convert_fusion, bf16[1024,4096]{1,0:T(8,128)(2,1)S(1)} %copy-done.1, pred[1024]{0:T(1024)(128)(4,1)S(1)} %get-tuple-element.5), kind=kOutput, calls=%fused_computation.4 | convolution fusion | flops 6449790976 | bytes 16253952 | tf_op jit(solution)/shard_map/dot_general | solution.py:48
  135.8 0.0 reduce-scatter.2.cloned.1.call-update
  135.8 0.1 dynamic_slice.3
  135.9 74.7 %reduce-scatter.2.cloned.1.call-done = bf16[768,512]{1,0:T(8,128)(2,1)} async-done(((bf16[768,4096]{1,0:T(8,128)(2,1)}), bf16[768,512]{1,0:T(8,128)(2,1)}) %reduce-scatter.2.cloned.1.call-update) | async-done | bytes 786448 | tf_op jit(solution)/shard_map/reduce_scatter | solution.py:50
  210.6 2.2 add_convert_fusion
  (7 shorter events, 0.0 us)
Async XLA Ops:
  6.5 2.9 %copy-start = (bf16[256,4096]{1,0:T(8,128)(2,1)S(1)}, bf16[256,4096]{1,0:T(8,128)(2,1)}, u32[]{:S(2)}) copy-start(bf16[256,4096]{1,0:T(8,128)(2,1)} %param.5) | copy-start | bytes 6291460
  6.5 85.8 %all-gather.2.cloned.1.call-start = ((), (), s32[]{:S(2)}) async-start(), calls=%async_computation.1 | async-start | bytes 17301504 | tf_op jit(solution)/shard_map/all_gather | solution.py:45
  11.7 198.9 %reduce-scatter.2.cloned.1.call-start = ((), (), s32[]{:S(2)}) async-start(), calls=%async_computation.2 | async-start | bytes 7077888 | tf_op jit(solution)/shard_map/reduce_scatter | solution.py:50
  92.3 23.0 %copy-start.2 = (f32[4096]{0:T(1024)S(1)}, f32[4096]{0:T(1024)}, u32[]{:S(2)}) copy-start(f32[4096]{0:T(1024)} %param.9) | copy-start | bytes 49156
  92.3 23.0 %copy-start.3 = (f32[1024]{0:T(1024)S(1)}, f32[1024]{0:T(1024)}, u32[]{:S(2)}) copy-start(f32[1024]{0:T(1024)} %param.8) | copy-start | bytes 12292
  115.3 11.7 %copy-start.1 = (bf16[1024,4096]{1,0:T(8,128)(2,1)S(1)}, bf16[1024,4096]{1,0:T(8,128)(2,1)}, u32[]{:S(2)}) copy-start(bf16[1024,4096]{1,0:T(8,128)(2,1)} %gather_fusion.1) | copy-start | bytes 25165828
Sparse Core Ops, SparseCore 0:
  11.8 80.4 all-gather.1
  135.9 74.6 reduce-scatter.1
where the time goes:
time: 221 us; the launch traced here: 220 us
  waiting for transfers between devices  155 us (70%)
  local copies, waits for them, and re-layouts  24 us (11%)
  matrix products  20.4 us (9%)
  between operations  13.5 us (6%)
  other arithmetic  6.37 us (3%)
    all_gather x1, waiting for transfers between devices, on_device(): collected = lax.all_gather(packed, 'buf', axis=0, tiled=True)  80.5 us
    reduce_scatter x1, waiting for transfers between devices, on_device(): lax.psum_scatter(rounded.astype(jnp.bfloat16), 'lat', scatter_dimension=1...  74.7 us
    gather x1, local copies, waits for them, and re-layouts, on_device(): all_units = jnp.take(collected, source * own_capacity + owner_rank, axis=0)  23 us
    dot_general x1, matrix products, encode_block(): lax.dot_general(centered, unit_block, (((1,), (1,)), ((), ())), preferred...  11.6 us
    dot_general x1, matrix products, on_device(): jnp.dot(active_all, all_units, preferred_element_type=jnp.float32)  8.79 us
  transfers between devices with their start and end apart: 2, of which 2 were waited for; matrix products, arithmetic and copies ran while one was open for 0% of the time, Pallas kernels for 0%

commit v1 on v0

v1 whole, which is shorter than its diff:
```python
import jax
import jax.numpy as jnp
from jax import lax
from jax.experimental import pallas as pl
from jax.experimental.pallas import tpu as pltpu
from jax.sharding import PartitionSpec as P

MESH = pl.DeviceIdType.MESH
NT = (((1,), (1,)), ((), ()))


def rem(value, size):
    return lax.rem(value, size)


def fused(
    rows_ref, buf_ref, win_hbm, scale_ref, bias_ref, out_ref,
    stage, send, recv, picked, units, cen, act, part, flow_r, flow_l,
    win_sem, own_sem, a2a_send, a2a_recv, ag_send, ag_recv, ag_recv2, rs_send, rs_recv,
):
    me = lax.axis_index("buf")
    owner = lax.axis_index("lat")
    core = rem(me, 2)
    chip = me // 2
    x, y = chip // 4, rem(chip, 4)
    a = x + core * (y - x)
    b = y + core * (x - y)
    right, left = rem(owner + 1, 8), rem(owner + 7, 8)

    barrier = pltpu.get_barrier_semaphore()

    def greet(k, carry):
        pl.semaphore_signal(
            barrier, inc=1, device_id={"buf": rem(me + k, 32)}, device_id_type=MESH
        )
        return carry

    lax.fori_loop(1, 32, greet, 0)
    for near in (right, left):
        pl.semaphore_signal(barrier, inc=1, device_id={"lat": near}, device_id_type=MESH)

    win_copy = pltpu.make_async_copy(win_hbm, cen, win_sem)
    win_copy.start()

    rows = rows_ref[...]
    offset = rows - me * 256
    mine = (offset >= 0) & (offset < 256)
    key = (lax.broadcasted_iota(jnp.int32, (32, 32), 1) * 256 + offset).astype(jnp.float32)
    first = jnp.min(jnp.where(mine, key, 8191.0), axis=1, keepdims=True).astype(jnp.int32)
    last = jnp.max(jnp.where(mine, key, 0.0), axis=1, keepdims=True).astype(jnp.int32)
    lane = lax.broadcasted_iota(jnp.int32, (32, 256), 1)
    for r, chosen in enumerate((first, last)):
        hot = (jnp.bitwise_and(chosen, 255) == lane).astype(jnp.float32).astype(jnp.bfloat16)
        for q in range(8):
            piece = jnp.dot(
                hot, buf_ref[:, q * 512:(q + 1) * 512], preferred_element_type=jnp.float32
            )
            for g in range(4):
                stage[g, pl.ds(r * 8 + q, 32, stride=16), :] = piece[:, g * 128:(g + 1) * 128]
    for g in range(4):
        send[:, g * 128:(g + 1) * 128] = stage[g].astype(jnp.bfloat16)

    pl.semaphore_wait(barrier, 33)

    def block_of(device):
        dc = rem(device, 2)
        dchip = device // 2
        dx, dy = dchip // 4, rem(dchip, 4)
        return dc * 16 + (dy + dc * (dx - dy)) * 4 + dx + dc * (dy - dx)

    def tile16(ref, index):
        return ref.at[pl.ds(pl.multiple_of(index * 16, 16), 16), :]

    def push(k, carry):
        target = rem(me + k, 32)
        pltpu.make_async_remote_copy(
            src_ref=tile16(send, block_of(target)),
            dst_ref=tile16(recv, me),
            send_sem=a2a_send,
            recv_sem=a2a_recv,
            device_id={"buf": target},
            device_id_type=MESH,
        ).start()
        return carry

    lax.fori_loop(1, 32, push, 0)
    my_block = core * 16 + b * 4 + a
    own_copy = pltpu.make_async_copy(tile16(send, my_block), tile16(recv, me), own_sem)
    own_copy.start()

    win_copy.wait()

    def center(t, carry):
        at = pl.ds(pl.multiple_of(t * 32, 32), 32)
        cen[at, :] = (cen[at, :].astype(jnp.float32) - bias_ref[...]).astype(jnp.bfloat16)
        return carry

    lax.fori_loop(0, 24, center, 0)

    own_copy.wait()
    pltpu.make_async_copy(recv.at[pl.ds(0, 496), :], recv.at[pl.ds(0, 496), :], a2a_recv).wait()

    own = jnp.broadcast_to(rows_ref[pl.ds(my_block, 1), :], (32, 32))
    own = lax.shift_right_logical(own, 8).astype(jnp.float32)
    entry = lax.broadcasted_iota(jnp.int32, (32, 32), 0)
    peer = lax.broadcasted_iota(jnp.int32, (32, 32), 1)
    source = jnp.sum(jnp.where(entry == peer, own, 0.0), axis=1, keepdims=True)
    twin = (own == source) & (peer < entry)
    rank = jnp.sum(jnp.where(twin, 1.0, 0.0), axis=1, keepdims=True)
    code = (source * 16.0 + rank * 8.0).astype(jnp.int32)
    code = jnp.concatenate([code + q for q in range(8)], axis=0)
    hot = code == lax.broadcasted_iota(jnp.int32, (256, 512), 1)
    hot = hot.astype(jnp.float32).astype(jnp.bfloat16)
    picked[...] = jnp.dot(hot, recv[...], preferred_element_type=jnp.float32)
    squares = jnp.zeros((32, 512), jnp.float32)
    for q in range(8):
        value = picked[q * 32:q * 32 + 32, :]
        squares += value * value
    inverse = lax.rsqrt(jnp.sum(squares, axis=1, keepdims=True) + 1e-06)
    mine_at = pl.ds(pl.multiple_of(my_block * 32, 32), 32)
    for q in range(8):
        value = picked[q * 32:q * 32 + 32, :]
        units[mine_at, q * 512:q * 512 + 512] = (value * inverse).astype(jnp.bfloat16)

    def block_at(da, db):
        return core * 16 + rem(b + db + 4, 4) * 4 + rem(a + da + 4, 4)

    def device_at(da, db):
        pa, pb = rem(a + da + 4, 4), rem(b + db + 4, 4)
        px, py = pa + core * (pb - pa), pb + core * (pa - pb)
        return (px * 4 + py) * 2 + core

    sibling = me + 1 - 2 * core
    sent = []

    def block_copy(block, target, count=32, half=0):
        at = units.at[pl.ds(pl.multiple_of(block * 32 + half * 16, 16), count), :]
        sem = ag_recv2 if half else ag_recv
        return pltpu.make_async_remote_copy(
            src_ref=at, dst_ref=at, send_sem=ag_send.at[len(sent)], recv_sem=sem.at[block],
            device_id={"buf": target}, device_id_type=MESH,
        )

    def give(block, target, count=32, half=0):
        copy = block_copy(block, target, count, half)
        copy.start()
        sent.append(copy)

    def arrive(block, count=32, half=0):
        at = units.at[pl.ds(pl.multiple_of(block * 32 + half * 16, 16), count), :]
        sem = ag_recv2 if half else ag_recv
        pltpu.make_async_copy(at, at, sem.at[block]).wait()

    def spread(block):
        give(block, device_at(0, 1))
        give(block, device_at(0, -1))
        give(block, sibling)

    give(my_block, device_at(1, 0))
    give(my_block, device_at(-1, 0))
    spread(my_block)

    block = block_at(-1, 0)
    arrive(block)
    give(block, device_at(1, 0), 16, 0)
    spread(block)
    block = block_at(1, 0)
    arrive(block)
    give(block, device_at(-1, 0), 16, 1)
    spread(block)

    def second(da):
        block = block_at(da, -1)
        arrive(block)
        give(block, device_at(0, 1), 16, 0)
        give(block, sibling)
        block = block_at(da, 1)
        arrive(block)
        give(block, device_at(0, -1), 16, 1)
        give(block, sibling)

    second(0)
    block = block_at(2, 0)
    arrive(block, 16, 0)
    arrive(block, 16, 1)
    spread(block)
    second(-1)
    second(1)
    second(2)

    def encode(group):
        at = pl.ds(pl.multiple_of(group * 256, 256), 256)
        scores = lax.dot_general(
            cen[...], units[at, :], NT, preferred_element_type=jnp.float32
        )
        act[:, at] = jnp.maximum(scores * scale_ref[:, at], 0.0).astype(jnp.bfloat16)

    other = 1 - core
    other_b = x + core * (y - x)
    mine_near = core * 2 + b // 2
    mine_far = core * 2 + 1 - b // 2
    other_near = other * 2 + other_b // 2
    other_far = other * 2 + 1 - other_b // 2

    def arrive_group(group):
        def one(i, carry):
            arrive(group * 8 + i)
            return carry

        lax.fori_loop(0, 8, one, 0)

    encode(mine_near)
    for da in (0, -1, 1, 2):
        block = block_at(da, 2)
        arrive(block, 16, 0)
        arrive(block, 16, 1)
        give(block, sibling)
    arrive_group(other_near)
    encode(other_near)
    encode(mine_far)
    arrive_group(other_far)
    encode(other_far)

    def decode(target):
        columns = pl.ds(pl.multiple_of(target * 512, 512), 512)
        value = jnp.dot(act[...], units[:, columns], preferred_element_type=jnp.float32)
        part[target] = value.astype(jnp.bfloat16)

    def half_of(ref, half):
        return ref.at[pl.ds(pl.multiple_of(half * 384, 384), 384), :]

    def rs_copy(i, source, flow, way):
        return pltpu.make_async_remote_copy(
            src_ref=source, dst_ref=flow.at[i],
            send_sem=rs_send.at[way, i], recv_sem=rs_recv.at[way, i],
            device_id={"lat": left if way else right}, device_id_type=MESH,
        )

    def rs_wait(i, flow, way):
        pltpu.make_async_copy(flow.at[i], flow.at[i], rs_recv.at[way, i]).wait()

    across = rem(owner + 4, 8)
    decode(across)
    rs_copy(0, half_of(part.at[across], 0), flow_r, 0).start()
    rs_copy(0, half_of(part.at[across], 1), flow_l, 1).start()

    def decode_pair(i, carry):
        decode(rem(owner + 3 + 2 * i, 8))
        return carry

    lax.fori_loop(0, 2, decode_pair, 0)
    rs_copy(1, half_of(part.at[rem(owner + 3, 8)], 1), flow_r, 0).start()
    rs_copy(1, half_of(part.at[rem(owner + 5, 8)], 0), flow_l, 1).start()

    def decode_rest(i, carry):
        decode(rem(owner + 6 + i, 8))
        return carry

    lax.fori_loop(0, 5, decode_rest, 0)

    def hop(i, carry):
        step = (i + 1) // 2
        for way, flow in ((0, flow_r), (1, flow_l)):
            half = rem(i + way, 2)
            target = rem(owner + 4 - step, 8) if way == 0 else rem(owner + 4 + step, 8)
            rs_wait(i - 2, flow, way)
            at = pl.ds(pl.multiple_of(half * 384, 384), 384)
            total = flow[i - 2].astype(jnp.float32) + part[target, at, :].astype(jnp.float32)
            flow[i - 2] = total.astype(jnp.bfloat16)
            rs_copy(i, flow.at[i - 2], flow, way).start()
        return carry

    lax.fori_loop(2, 7, hop, 0)

    bias = bias_ref[:, pl.ds(pl.multiple_of(owner * 512, 512), 512)]
    for i, j, half in ((5, 5, None), (6, 6, None)):
        rs_wait(i, flow_r, 0)
        rs_wait(j, flow_l, 1)
    for half in range(2):
        rows_at = slice(half * 384, half * 384 + 384)
        total = part[owner, rows_at, :].astype(jnp.float32) + bias
        total += flow_r[6 - half].astype(jnp.float32) + flow_l[5 + half].astype(jnp.float32)
        out_ref[rows_at, :] = total.astype(jnp.bfloat16)

    pltpu.make_async_copy(send.at[pl.ds(0, 496), :], send.at[pl.ds(0, 496), :], a2a_send).wait()
    for copy in sent:
        copy.wait_send()

    def drain(i, carry):
        for way in range(2):
            pltpu.make_async_copy(flow_r.at[i], flow_r.at[i], rs_send.at[way, i]).wait()
        return carry

    lax.fori_loop(0, 7, drain, 0)


def on_device(buffer, sample_rows, window, enc_scale, dec_bias):
    vmem = pl.BlockSpec(memory_space=pltpu.VMEM)
    call = pl.pallas_call(
        fused,
        out_shape=jax.ShapeDtypeStruct((768, 512), jnp.bfloat16),
        in_specs=[
            vmem, vmem, pl.BlockSpec(memory_space=pl.ANY), vmem, vmem,
        ],
        out_specs=vmem,
        scratch_shapes=[
            pltpu.VMEM((4, 512, 128), jnp.float32),
            pltpu.VMEM((512, 512), jnp.bfloat16),
            pltpu.VMEM((512, 512), jnp.bfloat16),
            pltpu.VMEM((256, 512), jnp.float32),
            pltpu.VMEM((1024, 4096), jnp.bfloat16),
            pltpu.VMEM((768, 4096), jnp.bfloat16),
            pltpu.VMEM((768, 1024), jnp.bfloat16),
            pltpu.VMEM((8, 768, 512), jnp.bfloat16),
            pltpu.VMEM((7, 384, 512), jnp.bfloat16),
            pltpu.VMEM((7, 384, 512), jnp.bfloat16),
            pltpu.SemaphoreType.DMA,
            pltpu.SemaphoreType.DMA,
            pltpu.SemaphoreType.DMA,
            pltpu.SemaphoreType.DMA,
            pltpu.SemaphoreType.DMA((40,)),
            pltpu.SemaphoreType.DMA((32,)),
            pltpu.SemaphoreType.DMA((32,)),
            pltpu.SemaphoreType.DMA((2, 7)),
            pltpu.SemaphoreType.DMA((2, 7)),
        ],
        compiler_params=pltpu.CompilerParams(
            collective_id=0, has_side_effects=True, vmem_limit_bytes=56 * 1024 * 1024
        ),
    )
    return call(
        sample_rows.reshape(32, 32), buffer, window,
        enc_scale.reshape(1, 1024), dec_bias.reshape(1, 4096),
    )


def solution(mesh):
    in_specs = (P("buf", None), P("lat"), P("buf", None), P("lat"), P())
    out_specs = P("buf", "lat")
    return jax.shard_map(
        on_device, mesh=mesh, in_specs=in_specs, out_specs=out_specs, check_vma=False
    )
```

time: 221 us -> 122 us (0.55)
  waiting for transfers between devices: 155 us -> 0 us
  Pallas kernels: 0 us -> 117 us
  local copies, waits for them, and re-layouts: 24 us -> 3.42 us
  matrix products: 20.4 us -> 0 us
  between operations: 13.5 us -> 0.01 us
  other arithmetic: 6.37 us -> 0 us
    pallas_call x0 -> x1, Pallas kernels: none -> 117 us  [on_device(): call(sample_rows.reshape(32, 32), buffer, window, enc_scale.reshape(1, 10...]
    all_gather x1 -> x0, waiting for transfers between devices: 80.5 us -> none  [on_device(): collected = lax.all_gather(packed, 'buf', axis=0, tiled=True)]
    reduce_scatter x1 -> x0, waiting for transfers between devices: 74.7 us -> none  [on_device(): lax.psum_scatter(rounded.astype(jnp.bfloat16), 'lat', scatter_dimension=1...]
    gather x2 -> x0, local copies, waits for them, and re-layouts: 23.9 us -> none  [the longest x1 23 us: on_device(): all_units = jnp.take(collected, source * own_capacity + owner_rank, axis=0)]
    dot_general x2 -> x0, matrix products: 20.4 us -> none  [the longest x1 11.6 us: encode_block(): lax.dot_general(centered, unit_block, (((1,), (1,)), ((), ())), preferred...]
    convert_element_type x2 -> x0, other arithmetic: 3.17 us -> none  [the longest x1 2.15 us: on_device(): return (summed + bias_part[None, :]).astype(jnp.bfloat16)]
  transfers between devices with their start and end apart: 2 -> 0, of which waited for: 2 -> 0; matrix products, arithmetic and copies ran while one was open for 0% -> 0% of each run, Pallas kernels for 0% -> 0%
where the time goes in v1:
time: 122 us; the launch traced here: 121 us
  Pallas kernels  117 us (96%)
  local copies, waits for them, and re-layouts  3.42 us (3%)
    pallas_call x1, Pallas kernels, on_device(): call(sample_rows.reshape(32, 32), buffer, window, enc_scale.reshape(1, 10...  117 us

profile of v1, /device:TPU:2, one launch (start us, length us, event | category | flops | bytes accessed | tf_op | source)
XLA Modules:
  0.0 120.7 jit_solution(14710196427618311589)
XLA Ops:
  0.0 1.4 %reshape.9.rows_ref = s32[32,32]{1,0:T(8,128)} reshape(s32[1024]{0:T(1024)} %param.6) | data formatting | bytes 8192 | tf_op jit(solution)/shard_map/reshape | solution.py:332
  1.4 117.3 %shard_map.55 = bf16[768,512]{1,0:T(8,128)(2,1)} custom-call(s32[32,32]{1,0:T(8,128)} %reshape.9.rows_ref, bf16[256,4096]{1,0:T(8,128)(2,1)} %buf_ref.1, bf16[768,4096]{1,0:T(8,128)(2,1)} %win_hbm.1, f32[1,1024]{1,0:T(1,128)} %bitcast.3, f32[1,4096]{1,0:T(1,128)} %bitcast.2), custom_call_target="tpu_custom_call" | custom-call | tf_op jit(solution)/shard_map/pallas_call | solution.py:331
  118.7 2.1 %copy.7 = bf16[768,512]{1,0:T(8,128)(2,1)} copy(bf16[768,512]{1,0:T(8,128)(2,1)} %shard_map.55) | data formatting | bytes 1572864

commit v2 on v1

v2 whole, which is shorter than its diff:
```python
import jax
import jax.numpy as jnp
from jax import lax
from jax.experimental import pallas as pl
from jax.experimental.pallas import tpu as pltpu
from jax.sharding import PartitionSpec as P

MESH = pl.DeviceIdType.MESH
NT = (((1,), (1,)), ((), ()))
ONE = 384
HALF = ONE // 2
SUB = 48


def rem(value, size):
    return lax.rem(value, size)


def fused(
    rows_ref, buf_hbm, win_hbm, scale_ref, bias_ref, out_ref,
    buf, stage, send, recv, picked, units, cen, cen_pair, act, act_pair,
    part, flow_r, flow_l, part_pair, pair_r, pair_l, scale_pair,
    in_sem, own_sem, a2a_send, a2a_recv, z_send, z_recv, ag_send, ag_recv, ag_recv2,
    rs_send, rs_recv, pair_send, pair_recv,
):
    me = lax.axis_index("buf")
    owner = lax.axis_index("lat")
    core = rem(me, 2)
    chip = me // 2
    x, y = chip // 4, rem(chip, 4)
    a = x + core * (y - x)
    b = y + core * (x - y)
    right, left, opposite = rem(owner + 1, 8), rem(owner + 7, 8), rem(owner + 4, 8)

    barrier = pltpu.get_barrier_semaphore()

    def greet(k, carry):
        pl.semaphore_signal(
            barrier, inc=1, device_id={"buf": rem(me + k, 32)}, device_id_type=MESH
        )
        return carry

    lax.fori_loop(1, 32, greet, 0)
    for near in (right, left, opposite):
        pl.semaphore_signal(barrier, inc=1, device_id={"lat": near}, device_id_type=MESH)

    buf_copy = pltpu.make_async_copy(buf_hbm, buf, own_sem)
    buf_copy.start()
    loads = [pltpu.make_async_copy(win_hbm.at[pl.ds(0, ONE), :], cen, in_sem.at[4])]
    for p in range(4):
        low = pl.multiple_of(ONE + rem(owner + 8 - p, 8) * SUB, 16)
        loads.append(pltpu.make_async_copy(
            win_hbm.at[pl.ds(low, SUB), :], cen_pair.at[pl.ds(p * SUB, SUB), :], in_sem.at[p]
        ))
    for load in loads:
        load.start()

    rows = rows_ref[...]
    offset = rows - me * 256
    mine = (offset >= 0) & (offset < 256)
    lanes = lax.broadcasted_iota(jnp.int32, (8, 128), 1)
    key = (lanes * 256 + offset).astype(jnp.float32)
    first, last = [], []
    for g in range(4):
        here = mine & (lanes >= g * 32) & (lanes < g * 32 + 32)
        first.append(jnp.min(jnp.where(here, key, 32767.0), axis=1, keepdims=True))
        last.append(jnp.max(jnp.where(here, key, 0.0), axis=1, keepdims=True))
    chosen = jnp.concatenate(first + last, axis=0).astype(jnp.int32)
    hot = jnp.bitwise_and(chosen, 255) == lax.broadcasted_iota(jnp.int32, (64, 256), 1)
    hot = hot.astype(jnp.float32).astype(jnp.bfloat16)
    buf_copy.wait()
    for q in range(8):
        piece = jnp.dot(
            hot, buf[:, q * 512:(q + 1) * 512], preferred_element_type=jnp.float32
        )
        for r in range(2):
            for g in range(4):
                stage[g, pl.ds(r * 8 + q, 32, stride=16), :] = (
                    piece[r * 32:r * 32 + 32, g * 128:(g + 1) * 128]
                )
    for g in range(4):
        send[:, g * 128:(g + 1) * 128] = stage[g].astype(jnp.bfloat16)

    pl.semaphore_wait(barrier, 34)

    def block_of(device):
        dc = rem(device, 2)
        dchip = device // 2
        dx, dy = dchip // 4, rem(dchip, 4)
        return dc * 16 + (dy + dc * (dx - dy)) * 4 + dx + dc * (dy - dx)

    def tile16(ref, index):
        return ref.at[pl.ds(pl.multiple_of(index * 16, 16), 16), :]

    def place(block):
        return rem(block, 4) * 8 + block // 4

    def push(k, carry):
        target = rem(me + k, 32)
        pltpu.make_async_remote_copy(
            src_ref=tile16(send, place(block_of(target))),
            dst_ref=tile16(recv, me),
            send_sem=a2a_send,
            recv_sem=a2a_recv,
            device_id={"buf": target},
            device_id_type=MESH,
        ).start()
        return carry

    lax.fori_loop(1, 32, push, 0)
    my_block = core * 16 + b * 4 + a
    own_copy = pltpu.make_async_copy(tile16(send, place(my_block)), tile16(recv, me), own_sem)
    own_copy.start()
    scale_copy = pltpu.make_async_remote_copy(
        src_ref=scale_ref, dst_ref=scale_pair, send_sem=z_send.at[0], recv_sem=z_recv.at[0],
        device_id={"lat": opposite}, device_id_type=MESH,
    )
    scale_copy.start()

    for load in loads:
        load.wait()

    def center(t, carry):
        at = pl.ds(pl.multiple_of(t * 32, 32), 32)
        cen[at, :] = (cen[at, :].astype(jnp.float32) - bias_ref[...]).astype(jnp.bfloat16)
        return carry

    def center_pair(t, carry):
        at = pl.ds(pl.multiple_of(t * 32, 32), 32)
        cen_pair[at, :] = (
            cen_pair[at, :].astype(jnp.float32) - bias_ref[...]
        ).astype(jnp.bfloat16)
        return carry

    lax.fori_loop(0, ONE // 32, center, 0)
    lax.fori_loop(0, 4 * SUB // 32, center_pair, 0)

    own_copy.wait()
    pltpu.make_async_copy(recv.at[pl.ds(0, 496), :], recv.at[pl.ds(0, 496), :], a2a_recv).wait()

    own = jnp.broadcast_to(rows_ref[pl.ds(my_block // 4, 1), :], (32, 128))
    own = lax.shift_right_logical(own, 8).astype(jnp.float32)
    entry = lax.broadcasted_iota(jnp.int32, (32, 128), 0)
    peer = lax.broadcasted_iota(jnp.int32, (32, 128), 1) - rem(my_block, 4) * 32
    source = jnp.sum(jnp.where(entry == peer, own, 0.0), axis=1, keepdims=True)
    twin = (own == source) & (peer >= 0) & (peer < entry)
    rank = jnp.sum(jnp.where(twin, 1.0, 0.0), axis=1, keepdims=True)
    code = (source * 16.0 + rank * 8.0).astype(jnp.int32)
    code = jnp.concatenate([code + q for q in range(8)], axis=0)
    hot = code == lax.broadcasted_iota(jnp.int32, (256, 512), 1)
    hot = hot.astype(jnp.float32).astype(jnp.bfloat16)
    picked[...] = jnp.dot(hot, recv[...], preferred_element_type=jnp.float32)
    squares = jnp.zeros((32, 512), jnp.float32)
    for q in range(8):
        value = picked[q * 32:q * 32 + 32, :]
        squares += value * value
    inverse = lax.rsqrt(jnp.sum(squares, axis=1, keepdims=True) + 1e-06)
    mine_at = pl.ds(pl.multiple_of(my_block * 32, 32), 32)
    for q in range(8):
        value = picked[q * 32:q * 32 + 32, :]
        units[0, mine_at, q * 512:q * 512 + 512] = (value * inverse).astype(jnp.bfloat16)

    def block_at(da, db):
        return core * 16 + rem(b + db + 4, 4) * 4 + rem(a + da + 4, 4)

    def device_at(da, db):
        pa, pb = rem(a + da + 4, 4), rem(b + db + 4, 4)
        px, py = pa + core * (pb - pa), pb + core * (pa - pb)
        return (px * 4 + py) * 2 + core

    sibling = me + 1 - 2 * core
    sent = [[], []]

    def block_ref(w, block, count=32, half=0):
        return units.at[w, pl.ds(pl.multiple_of(block * 32 + half * 16, 16), count), :]

    def give(w, block, target, count=32, half=0):
        at = block_ref(w, block, count, half)
        sem = ag_recv2 if half else ag_recv
        copy = pltpu.make_async_remote_copy(
            src_ref=at, dst_ref=at, send_sem=ag_send.at[w, len(sent[w])],
            recv_sem=sem.at[w, block], device_id={"buf": target}, device_id_type=MESH,
        )
        copy.start()
        sent[w].append(copy)

    def arrive(w, block, count=32, half=0):
        at = block_ref(w, block, count, half)
        sem = ag_recv2 if half else ag_recv
        pltpu.make_async_copy(at, at, sem.at[w, block]).wait()

    def spread(w, block):
        give(w, block, device_at(0, 1))
        give(w, block, device_at(0, -1))
        give(w, block, sibling)

    def second(w, da):
        block = block_at(da, -1)
        arrive(w, block)
        give(w, block, device_at(0, 1), 16, 0)
        give(w, block, sibling)
        block = block_at(da, 1)
        arrive(w, block)
        give(w, block, device_at(0, -1), 16, 1)
        give(w, block, sibling)

    def far(w, da):
        block = block_at(da, 2)
        arrive(w, block, 16, 0)
        arrive(w, block, 16, 1)
        give(w, block, sibling)

    def step(w, n):
        if n == 0:
            give(w, my_block, device_at(1, 0))
            give(w, my_block, device_at(-1, 0))
            spread(w, my_block)
        elif n == 1:
            block = block_at(-1, 0)
            arrive(w, block)
            give(w, block, device_at(1, 0), 16, 0)
            spread(w, block)
        elif n == 2:
            block = block_at(1, 0)
            arrive(w, block)
            give(w, block, device_at(-1, 0), 16, 1)
            spread(w, block)
        elif n == 3:
            second(w, 0)
        elif n == 4:
            block = block_at(2, 0)
            arrive(w, block, 16, 0)
            arrive(w, block, 16, 1)
            spread(w, block)
        elif n < 8:
            second(w, (-1, 1, 2)[n - 5])
        else:
            far(w, (0, -1, 1, 2)[n - 8])

    step(0, 0)
    z_copy = pltpu.make_async_remote_copy(
        src_ref=block_ref(0, my_block), dst_ref=block_ref(1, my_block),
        send_sem=z_send.at[1], recv_sem=z_recv.at[1],
        device_id={"lat": opposite}, device_id_type=MESH,
    )
    z_copy.start()
    for n in range(1, 8):
        step(0, n)

    def encode(group):
        at = pl.ds(pl.multiple_of(group * 256, 256), 256)
        scores = lax.dot_general(
            cen[...], units[0, at, :], NT, preferred_element_type=jnp.float32
        )
        act[:, at] = jnp.maximum(scores * scale_ref[:, at], 0.0).astype(jnp.bfloat16)

    def encode_pair(w, group):
        at = pl.ds(pl.multiple_of(group * 256, 256), 256)
        scale = (scale_pair if w else scale_ref)[:, at]
        scores = lax.dot_general(
            cen_pair[...], units[w, at, :], NT, preferred_element_type=jnp.float32
        )
        act_pair[w, :, at] = jnp.maximum(scores * scale, 0.0).astype(jnp.bfloat16)

    other = 1 - core
    other_b = x + core * (y - x)
    mine_near = core * 2 + b // 2
    mine_far = core * 2 + 1 - b // 2
    other_near = other * 2 + other_b // 2
    other_far = other * 2 + 1 - other_b // 2

    def arrive_group(w, group):
        def one(i, carry):
            arrive(w, group * 8 + i)
            return carry

        lax.fori_loop(0, 8, one, 0)

    encode(mine_near)
    for n in range(8, 12):
        step(0, n)
    arrive_group(0, other_near)
    encode(other_near)
    encode(mine_far)
    arrive_group(0, other_far)
    encode(other_far)

    def decode(target):
        columns = pl.ds(pl.multiple_of(target * 512, 512), 512)
        value = jnp.dot(act[...], units[0, :, columns], preferred_element_type=jnp.float32)
        part[target] = value.astype(jnp.bfloat16)

    def half_of(ref, half):
        return ref.at[pl.ds(half * HALF, HALF), :]

    def rs_copy(i, source, flow, way):
        return pltpu.make_async_remote_copy(
            src_ref=source, dst_ref=flow.at[i],
            send_sem=rs_send.at[way, i], recv_sem=rs_recv.at[way, i],
            device_id={"lat": left if way else right}, device_id_type=MESH,
        )

    def rs_wait(i, flow, way):
        pltpu.make_async_copy(flow.at[i], flow.at[i], rs_recv.at[way, i]).wait()

    def hop(i):
        for way, flow in ((0, flow_r), (1, flow_l)):
            low = ((i + way) % 2) * HALF
            away = 4 - (i + 1) // 2
            target = rem(owner + (8 - away if way else away), 8)
            rs_wait(i - 2, flow, way)
            total = flow[i - 2].astype(jnp.float32)
            total += part[target, low:low + HALF, :].astype(jnp.float32)
            flow[i - 2] = total.astype(jnp.bfloat16)
            rs_copy(i, flow.at[i - 2], flow, way).start()

    decode(opposite)
    rs_copy(0, half_of(part.at[opposite], 0), flow_r, 0).start()
    rs_copy(0, half_of(part.at[opposite], 1), flow_l, 1).start()
    z_copy.wait_recv()
    step(1, 0)

    def decode_next(i, carry):
        decode(rem(owner + 3 + 2 * i, 8))
        return carry

    lax.fori_loop(0, 2, decode_next, 0)
    rs_copy(1, half_of(part.at[rem(owner + 3, 8)], 1), flow_r, 0).start()
    rs_copy(1, half_of(part.at[rem(owner + 5, 8)], 0), flow_l, 1).start()
    step(1, 1)
    step(1, 2)

    def decode_rest(i, carry):
        decode(rem(owner + 6 + i, 8))
        return carry

    lax.fori_loop(0, 5, decode_rest, 0)
    step(1, 3)
    hop(2)
    step(1, 4)
    step(1, 5)
    lax.fori_loop(0, 4, lambda i, carry: (encode_pair(0, i), carry)[1], 0)
    hop(3)
    step(1, 6)
    step(1, 7)
    scale_copy.wait_recv()
    encode_pair(1, mine_near)
    hop(4)
    for n in range(8, 12):
        step(1, n)
    arrive_group(1, other_near)
    encode_pair(1, other_near)
    encode_pair(1, mine_far)
    hop(5)
    arrive_group(1, other_far)
    encode_pair(1, other_far)
    hop(6)

    def decode_pair(o, carry):
        columns = pl.ds(pl.multiple_of(rem(owner + o, 8) * 512, 512), 512)
        value = jnp.dot(act_pair[0], units[0, :, columns], preferred_element_type=jnp.float32)
        value += jnp.dot(act_pair[1], units[1, :, columns], preferred_element_type=jnp.float32)
        value = value.astype(jnp.bfloat16)
        for p in range(4):
            part_pair[p, o] = value[p * SUB:(p + 1) * SUB, :]
        return carry

    def pair_copy(way, p, source):
        flow = pair_l if way else pair_r
        return pltpu.make_async_remote_copy(
            src_ref=source, dst_ref=flow.at[p, pl.ds(0, 5 - p)],
            send_sem=pair_send.at[way, p], recv_sem=pair_recv.at[way, p],
            device_id={"lat": left if way else right}, device_id_type=MESH,
        )

    def pair_wait(way, p):
        flow = pair_l if way else pair_r
        at = flow.at[p, pl.ds(0, 5 - p)]
        pltpu.make_async_copy(at, at, pair_recv.at[way, p]).wait()

    lax.fori_loop(1, 8, decode_pair, 0)
    pair_copies = [pair_copy(0, 0, part_pair.at[0, pl.ds(1, 5)])]
    pair_copies.append(pair_copy(1, 0, part_pair.at[3, pl.ds(3, 5)]))
    for copy in pair_copies:
        copy.start()
    decode_pair(0, 0)

    bias = bias_ref[:, pl.ds(pl.multiple_of(owner * 512, 512), 512)]
    for i in (5, 6):
        rs_wait(i, flow_r, 0)
        rs_wait(i, flow_l, 1)
    for half in range(2):
        at = slice(half * HALF, half * HALF + HALF)
        total = part[owner, at, :].astype(jnp.float32) + bias
        total += flow_r[6 - half].astype(jnp.float32) + flow_l[5 + half].astype(jnp.float32)
        out_ref[at, :] = total.astype(jnp.bfloat16)

    for p in range(1, 5):
        for way, flow in ((0, pair_r), (1, pair_l)):
            pair_wait(way, p - 1)
            low = 0 if way else 1
            if p < 4:
                for k in range(5 - p):
                    mine_part = part_pair[3 - p, 3 + p + k] if way else part_pair[p, 1 + k]
                    total = flow[p - 1, low + k].astype(jnp.float32)
                    total += mine_part.astype(jnp.float32)
                    flow[p - 1, low + k] = total.astype(jnp.bfloat16)
            copy = pair_copy(way, p, flow.at[p - 1, pl.ds(low, 5 - p)])
            copy.start()
            pair_copies.append(copy)
    for way in range(2):
        pair_wait(way, 4)

    for r in range(-4, 4):
        terms = []
        if -3 <= r <= 0:
            terms.append(part_pair[-r, 0])
        for p in range(5):
            if (r + 1 + p) % 8 == 0:
                terms.append(pair_r[p, 0])
            if (r + 2 - p) % 8 == 0:
                terms.append(pair_l[p, 4 - p])
        total = jnp.broadcast_to(bias, (SUB, 512))
        for term in terms:
            total += term.astype(jnp.float32)
        low = pl.multiple_of(ONE + rem(owner + 8 + r, 8) * SUB, 16)
        out_ref[pl.ds(low, SUB), :] = total.astype(jnp.bfloat16)

    pltpu.make_async_copy(send.at[pl.ds(0, 496), :], send.at[pl.ds(0, 496), :], a2a_send).wait()
    for copy in [scale_copy, z_copy] + sent[0] + sent[1] + pair_copies:
        copy.wait_send()

    def drain(i, carry):
        for way in range(2):
            pltpu.make_async_copy(flow_r.at[i], flow_r.at[i], rs_send.at[way, i]).wait()
        return carry

    lax.fori_loop(0, 7, drain, 0)


def on_device(buffer, sample_rows, window, enc_scale, dec_bias):
    vmem = pl.BlockSpec(memory_space=pltpu.VMEM)
    anywhere = pl.BlockSpec(memory_space=pl.ANY)
    call = pl.pallas_call(
        fused,
        out_shape=jax.ShapeDtypeStruct((768, 512), jnp.bfloat16),
        in_specs=[vmem, anywhere, anywhere, vmem, vmem],
        out_specs=vmem,
        scratch_shapes=[
            pltpu.VMEM((256, 4096), jnp.bfloat16),
            pltpu.VMEM((4, 512, 128), jnp.float32),
            pltpu.VMEM((512, 512), jnp.bfloat16),
            pltpu.VMEM((512, 512), jnp.bfloat16),
            pltpu.VMEM((256, 512), jnp.float32),
            pltpu.VMEM((2, 1024, 4096), jnp.bfloat16),
            pltpu.VMEM((ONE, 4096), jnp.bfloat16),
            pltpu.VMEM((4 * SUB, 4096), jnp.bfloat16),
            pltpu.VMEM((ONE, 1024), jnp.bfloat16),
            pltpu.VMEM((2, 4 * SUB, 1024), jnp.bfloat16),
            pltpu.VMEM((8, ONE, 512), jnp.bfloat16),
            pltpu.VMEM((7, HALF, 512), jnp.bfloat16),
            pltpu.VMEM((7, HALF, 512), jnp.bfloat16),
            pltpu.VMEM((4, 8, SUB, 512), jnp.bfloat16),
            pltpu.VMEM((5, 5, SUB, 512), jnp.bfloat16),
            pltpu.VMEM((5, 5, SUB, 512), jnp.bfloat16),
            pltpu.VMEM((1, 1024), jnp.float32),
            pltpu.SemaphoreType.DMA((5,)),
            pltpu.SemaphoreType.DMA,
            pltpu.SemaphoreType.DMA,
            pltpu.SemaphoreType.DMA,
            pltpu.SemaphoreType.DMA((2,)),
            pltpu.SemaphoreType.DMA((2,)),
            pltpu.SemaphoreType.DMA((2, 40)),
            pltpu.SemaphoreType.DMA((2, 32)),
            pltpu.SemaphoreType.DMA((2, 32)),
            pltpu.SemaphoreType.DMA((2, 7)),
            pltpu.SemaphoreType.DMA((2, 7)),
            pltpu.SemaphoreType.DMA((2, 5)),
            pltpu.SemaphoreType.DMA((2, 5)),
        ],
        compiler_params=pltpu.CompilerParams(
            collective_id=0, has_side_effects=True, vmem_limit_bytes=56 * 1024 * 1024
        ),
    )
    return call(
        sample_rows.reshape(8, 128), buffer, window,
        enc_scale.reshape(1, 1024), dec_bias.reshape(1, 4096),
    )


def solution(mesh):
    in_specs = (P("buf", None), P("lat"), P("buf", None), P("lat"), P())
    out_specs = P("buf", "lat")
    return jax.shard_map(
        on_device, mesh=mesh, in_specs=in_specs, out_specs=out_specs, check_vma=False
    )
```

time: 122 us -> 116 us (0.951)
  Pallas kernels: 117 us -> 113 us
  local copies, waits for them, and re-layouts: 3.42 us -> 2.06 us
    pallas_call x1, Pallas kernels: 117 us -> 113 us  [on_device(): call(sample_rows.reshape(8, 128), buffer, window, enc_scale.reshape(1, 10...]
    reshape x1 -> x0, local copies, waits for them, and re-layouts: 1.36 us -> none  [on_device(): sample_rows.reshape(32, 32)]
where the time goes in v2:
time: 116 us; the launch traced here: 115 us
  Pallas kernels  113 us (97%)
  local copies, waits for them, and re-layouts  2.06 us (2%)
    pallas_call x1, Pallas kernels, on_device(): call(sample_rows.reshape(8, 128), buffer, window, enc_scale.reshape(1, 10...  113 us

profile of v2, /device:TPU:2, one launch (start us, length us, event | category | flops | bytes accessed | tf_op | source)
XLA Modules:
  0.0 115.1 jit_solution(851217627424457310)
XLA Ops:
  0.0 113.0 %shard_map.55 = bf16[768,512]{1,0:T(8,128)(2,1)} custom-call(s32[8,128]{1,0:T(8,128)} %bitcast.4, bf16[256,4096]{1,0:T(8,128)(2,1)} %buf_hbm.1, bf16[768,4096]{1,0:T(8,128)(2,1)} %win_hbm.1, f32[1,1024]{1,0:T(1,128)} %bitcast.5, f32[1,4096]{1,0:T(1,128)} %bitcast.3), custom_call_target="tpu_custom_call" | custom-call | tf_op jit(solution)/shard_map/pallas_call | solution.py:485
  113.0 2.1 %copy.7 = bf16[768,512]{1,0:T(8,128)(2,1)} copy(bf16[768,512]{1,0:T(8,128)(2,1)} %shard_map.55) | data formatting | bytes 1572864

commit v3 on v2

--- a/solution.py
+++ b/solution.py
@@ -9,7 +9,8 @@
 NT = (((1,), (1,)), ((), ()))
 ONE = 384
 HALF = ONE // 2
-SUB = 48
+PIECES = 3
+SUB = 16 * PIECES
 
 
 def rem(value, size):
@@ -19,8 +20,8 @@
 def fused(
     rows_ref, buf_hbm, win_hbm, scale_ref, bias_ref, out_ref,
     buf, stage, send, recv, picked, units, cen, cen_pair, act, act_pair,
-    part, flow_r, flow_l, part_pair, pair_r, pair_l, scale_pair,
-    in_sem, own_sem, a2a_send, a2a_recv, z_send, z_recv, ag_send, ag_recv, ag_recv2,
+    part, flow_r, flow_l, part_pair, pair_flow, pair_far, scale_pair,
+    in_sem, own_sem, a2a_send, a2a_recv, z_send, z_recv, ag_send, ag_recv,
     rs_send, rs_recv, pair_send, pair_recv,
 ):
     me = lax.axis_index("buf")
@@ -41,8 +42,8 @@
         return carry
 
     lax.fori_loop(1, 32, greet, 0)
-    for near in (right, left, opposite):
-        pl.semaphore_signal(barrier, inc=1, device_id={"lat": near}, device_id_type=MESH)
+    for k in (1, 2, 4, 6, 7):
+        pl.semaphore_signal(barrier, inc=1, device_id={"lat": rem(owner + k, 8)}, device_id_type=MESH)
 
     buf_copy = pltpu.make_async_copy(buf_hbm, buf, own_sem)
     buf_copy.start()
@@ -81,13 +82,13 @@
     for g in range(4):
         send[:, g * 128:(g + 1) * 128] = stage[g].astype(jnp.bfloat16)
 
-    pl.semaphore_wait(barrier, 34)
+    pl.semaphore_wait(barrier, 36)
 
     def block_of(device):
         dc = rem(device, 2)
         dchip = device // 2
         dx, dy = dchip // 4, rem(dchip, 4)
-        return dc * 16 + (dy + dc * (dx - dy)) * 4 + dx + dc * (dy - dx)
+        return dc * 16 + (dx + dc * (dy - dx)) * 4 + dy + dc * (dx - dy)
 
     def tile16(ref, index):
         return ref.at[pl.ds(pl.multiple_of(index * 16, 16), 16), :]
@@ -96,7 +97,9 @@
         return rem(block, 4) * 8 + block // 4
 
     def push(k, carry):
-        target = rem(me + k, 32)
+        far = 32 - k
+        tx, ty = rem(x + far // 8, 4), rem(y + rem(far, 8) // 2, 4)
+        target = (tx * 4 + ty) * 2 + rem(core + far, 2)
         pltpu.make_async_remote_copy(
             src_ref=tile16(send, place(block_of(target))),
             dst_ref=tile16(recv, me),
@@ -108,7 +111,7 @@
         return carry
 
     lax.fori_loop(1, 32, push, 0)
-    my_block = core * 16 + b * 4 + a
+    my_block = core * 16 + a * 4 + b
     own_copy = pltpu.make_async_copy(tile16(send, place(my_block)), tile16(recv, me), own_sem)
     own_copy.start()
     scale_copy = pltpu.make_async_remote_copy(
@@ -161,7 +164,7 @@
         units[0, mine_at, q * 512:q * 512 + 512] = (value * inverse).astype(jnp.bfloat16)
 
     def block_at(da, db):
-        return core * 16 + rem(b + db + 4, 4) * 4 + rem(a + da + 4, 4)
+        return core * 16 + rem(a + da + 4, 4) * 4 + rem(b + db + 4, 4)
 
     def device_at(da, db):
         pa, pb = rem(a + da + 4, 4), rem(b + db + 4, 4)
@@ -171,71 +174,44 @@
     sibling = me + 1 - 2 * core
     sent = [[], []]
 
-    def block_ref(w, block, count=32, half=0):
-        return units.at[w, pl.ds(pl.multiple_of(block * 32 + half * 16, 16), count), :]
-
-    def give(w, block, target, count=32, half=0):
-        at = block_ref(w, block, count, half)
-        sem = ag_recv2 if half else ag_recv
+    mate = 1 - 2 * rem(a, 2)
+
+    def block_ref(w, block):
+        return units.at[w, pl.ds(pl.multiple_of(block * 32, 32), 32), :]
+
+    def give(w, block, target):
+        at = block_ref(w, block)
         copy = pltpu.make_async_remote_copy(
             src_ref=at, dst_ref=at, send_sem=ag_send.at[w, len(sent[w])],
-            recv_sem=sem.at[w, block], device_id={"buf": target}, device_id_type=MESH,
+            recv_sem=ag_recv.at[w, block], device_id={"buf": target}, device_id_type=MESH,
         )
         copy.start()
         sent[w].append(copy)
 
-    def arrive(w, block, count=32, half=0):
-        at = block_ref(w, block, count, half)
-        sem = ag_recv2 if half else ag_recv
-        pltpu.make_async_copy(at, at, sem.at[w, block]).wait()
+    def arrive(w, block):
+        at = block_ref(w, block)
+        pltpu.make_async_copy(at, at, ag_recv.at[w, block]).wait()
 
     def spread(w, block):
-        give(w, block, device_at(0, 1))
-        give(w, block, device_at(0, -1))
+        for db in (2, 1, -1):
+            give(w, block, device_at(0, db))
         give(w, block, sibling)
 
-    def second(w, da):
-        block = block_at(da, -1)
-        arrive(w, block)
-        give(w, block, device_at(0, 1), 16, 0)
-        give(w, block, sibling)
-        block = block_at(da, 1)
-        arrive(w, block)
-        give(w, block, device_at(0, -1), 16, 1)
-        give(w, block, sibling)
-
-    def far(w, da):
-        block = block_at(da, 2)
-        arrive(w, block, 16, 0)
-        arrive(w, block, 16, 1)
-        give(w, block, sibling)
-
     def step(w, n):
+        da = (0, mate, -mate, 2)[n % 4]
         if n == 0:
-            give(w, my_block, device_at(1, 0))
-            give(w, my_block, device_at(-1, 0))
+            for da in (mate, 2, -mate):
+                give(w, my_block, device_at(da, 0))
             spread(w, my_block)
-        elif n == 1:
-            block = block_at(-1, 0)
+        elif n < 4:
+            block = block_at(da, 0)
             arrive(w, block)
-            give(w, block, device_at(1, 0), 16, 0)
             spread(w, block)
-        elif n == 2:
-            block = block_at(1, 0)
-            arrive(w, block)
-            give(w, block, device_at(-1, 0), 16, 1)
-            spread(w, block)
-        elif n == 3:
-            second(w, 0)
-        elif n == 4:
-            block = block_at(2, 0)
-            arrive(w, block, 16, 0)
-            arrive(w, block, 16, 1)
-            spread(w, block)
-        elif n < 8:
-            second(w, (-1, 1, 2)[n - 5])
         else:
-            far(w, (0, -1, 1, 2)[n - 8])
+            for db in (1, -1, 2):
+                block = block_at(da, db)
+                arrive(w, block)
+                give(w, block, sibling)
 
     step(0, 0)
     z_copy = pltpu.make_async_remote_copy(
@@ -244,7 +220,7 @@
         device_id={"lat": opposite}, device_id_type=MESH,
     )
     z_copy.start()
-    for n in range(1, 8):
+    for n in range(1, 6):
         step(0, n)
 
     def encode(group):
@@ -263,11 +239,11 @@
         act_pair[w, :, at] = jnp.maximum(scores * scale, 0.0).astype(jnp.bfloat16)
 
     other = 1 - core
-    other_b = x + core * (y - x)
-    mine_near = core * 2 + b // 2
-    mine_far = core * 2 + 1 - b // 2
-    other_near = other * 2 + other_b // 2
-    other_far = other * 2 + 1 - other_b // 2
+    other_a = y + core * (x - y)
+    mine_near = core * 2 + a // 2
+    mine_far = core * 2 + 1 - a // 2
+    other_near = other * 2 + other_a // 2
+    other_far = other * 2 + 1 - other_a // 2
 
     def arrive_group(w, group):
         def one(i, carry):
@@ -277,10 +253,12 @@
         lax.fori_loop(0, 8, one, 0)
 
     encode(mine_near)
-    for n in range(8, 12):
-        step(0, n)
+    step(0, 6)
     arrive_group(0, other_near)
     encode(other_near)
+    step(0, 7)
+    z_copy.wait_recv()
+    step(1, 0)
     encode(mine_far)
     arrive_group(0, other_far)
     encode(other_far)
@@ -317,8 +295,6 @@
     decode(opposite)
     rs_copy(0, half_of(part.at[opposite], 0), flow_r, 0).start()
     rs_copy(0, half_of(part.at[opposite], 1), flow_l, 1).start()
-    z_copy.wait_recv()
-    step(1, 0)
 
     def decode_next(i, carry):
         decode(rem(owner + 3 + 2 * i, 8))
@@ -327,31 +303,28 @@
     lax.fori_loop(0, 2, decode_next, 0)
     rs_copy(1, half_of(part.at[rem(owner + 3, 8)], 1), flow_r, 0).start()
     rs_copy(1, half_of(part.at[rem(owner + 5, 8)], 0), flow_l, 1).start()
-    step(1, 1)
-    step(1, 2)
+    for n in range(1, 4):
+        step(1, n)
 
     def decode_rest(i, carry):
         decode(rem(owner + 6 + i, 8))
         return carry
 
     lax.fori_loop(0, 5, decode_rest, 0)
-    step(1, 3)
+    step(1, 4)
     hop(2)
-    step(1, 4)
+    lax.fori_loop(0, 4, lambda i, carry: (encode_pair(0, i), carry)[1], 0)
     step(1, 5)
-    lax.fori_loop(0, 4, lambda i, carry: (encode_pair(0, i), carry)[1], 0)
     hop(3)
-    step(1, 6)
-    step(1, 7)
     scale_copy.wait_recv()
     encode_pair(1, mine_near)
     hop(4)
-    for n in range(8, 12):
-        step(1, n)
+    step(1, 6)
     arrive_group(1, other_near)
     encode_pair(1, other_near)
+    hop(5)
+    step(1, 7)
     encode_pair(1, mine_far)
-    hop(5)
     arrive_group(1, other_far)
     encode_pair(1, other_far)
     hop(6)
@@ -362,69 +335,92 @@
         value += jnp.dot(act_pair[1], units[1, :, columns], preferred_element_type=jnp.float32)
         value = value.astype(jnp.bfloat16)
         for p in range(4):
-            part_pair[p, o] = value[p * SUB:(p + 1) * SUB, :]
-        return carry
-
-    def pair_copy(way, p, source):
-        flow = pair_l if way else pair_r
-        return pltpu.make_async_remote_copy(
-            src_ref=source, dst_ref=flow.at[p, pl.ds(0, 5 - p)],
-            send_sem=pair_send.at[way, p], recv_sem=pair_recv.at[way, p],
-            device_id={"lat": left if way else right}, device_id_type=MESH,
-        )
-
-    def pair_wait(way, p):
-        flow = pair_l if way else pair_r
-        at = flow.at[p, pl.ds(0, 5 - p)]
-        pltpu.make_async_copy(at, at, pair_recv.at[way, p]).wait()
+            for c in range(PIECES):
+                low = p * SUB + c * 16
+                part_pair[c, p, o] = value[low:low + 16, :]
+        return carry
+
+    pair_copies = []
+
+    def pair_give(way, c, p, source, dest, distance=1, slot=None):
+        slot = p if slot is None else slot
+        copy = pltpu.make_async_remote_copy(
+            src_ref=source, dst_ref=dest,
+            send_sem=pair_send.at[way, c, slot], recv_sem=pair_recv.at[way, c, slot],
+            device_id={"lat": rem(owner + (8 - distance if way else distance), 8)},
+            device_id_type=MESH,
+        )
+        copy.start()
+        pair_copies.append(copy)
+
+    def pair_wait(way, c, p):
+        if p == 4:
+            at = pair_far.at[way, c]
+        else:
+            at = pair_flow.at[way, c, p, pl.ds(0, 5 - p if p < 3 else 1)]
+        pltpu.make_async_copy(at, at, pair_recv.at[way, c, p]).wait()
 
     lax.fori_loop(1, 8, decode_pair, 0)
-    pair_copies = [pair_copy(0, 0, part_pair.at[0, pl.ds(1, 5)])]
-    pair_copies.append(pair_copy(1, 0, part_pair.at[3, pl.ds(3, 5)]))
-    for copy in pair_copies:
-        copy.start()
+    for c in range(PIECES):
+        for way in range(2):
+            source = part_pair.at[c, 3 if way else 0, pl.ds(3 if way else 1, 5)]
+            pair_give(way, c, 0, source, pair_flow.at[way, c, 0])
     decode_pair(0, 0)
 
     bias = bias_ref[:, pl.ds(pl.multiple_of(owner * 512, 512), 512)]
-    for i in (5, 6):
-        rs_wait(i, flow_r, 0)
-        rs_wait(i, flow_l, 1)
-    for half in range(2):
-        at = slice(half * HALF, half * HALF + HALF)
-        total = part[owner, at, :].astype(jnp.float32) + bias
-        total += flow_r[6 - half].astype(jnp.float32) + flow_l[5 + half].astype(jnp.float32)
-        out_ref[at, :] = total.astype(jnp.bfloat16)
-
-    for p in range(1, 5):
-        for way, flow in ((0, pair_r), (1, pair_l)):
-            pair_wait(way, p - 1)
-            low = 0 if way else 1
-            if p < 4:
+
+    def finish_one():
+        for i in (5, 6):
+            rs_wait(i, flow_r, 0)
+            rs_wait(i, flow_l, 1)
+        for half in range(2):
+            at = slice(half * HALF, half * HALF + HALF)
+            total = part[owner, at, :].astype(jnp.float32) + bias
+            total += flow_r[6 - half].astype(jnp.float32) + flow_l[5 + half].astype(jnp.float32)
+            out_ref[at, :] = total.astype(jnp.bfloat16)
+
+    for p in range(1, 4):
+        for c in range(PIECES):
+            for way in range(2):
+                pair_wait(way, c, p - 1)
+                low = 0 if way else 1
                 for k in range(5 - p):
-                    mine_part = part_pair[3 - p, 3 + p + k] if way else part_pair[p, 1 + k]
-                    total = flow[p - 1, low + k].astype(jnp.float32)
+                    mine_part = part_pair[c, 3 - p, 3 + p + k] if way else part_pair[c, p, 1 + k]
+                    total = pair_flow[way, c, p - 1, low + k].astype(jnp.float32)
                     total += mine_part.astype(jnp.float32)
-                    flow[p - 1, low + k] = total.astype(jnp.bfloat16)
-            copy = pair_copy(way, p, flow.at[p - 1, pl.ds(low, 5 - p)])
-            copy.start()
-            pair_copies.append(copy)
-    for way in range(2):
-        pair_wait(way, 4)
-
-    for r in range(-4, 4):
-        terms = []
-        if -3 <= r <= 0:
-            terms.append(part_pair[-r, 0])
-        for p in range(5):
-            if (r + 1 + p) % 8 == 0:
-                terms.append(pair_r[p, 0])
-            if (r + 2 - p) % 8 == 0:
-                terms.append(pair_l[p, 4 - p])
-        total = jnp.broadcast_to(bias, (SUB, 512))
-        for term in terms:
-            total += term.astype(jnp.float32)
-        low = pl.multiple_of(ONE + rem(owner + 8 + r, 8) * SUB, 16)
-        out_ref[pl.ds(low, SUB), :] = total.astype(jnp.bfloat16)
+                    pair_flow[way, c, p - 1, low + k] = total.astype(jnp.bfloat16)
+                source = pair_flow.at[way, c, p - 1, pl.ds(low, 5 - p)]
+                if p < 3:
+                    pair_give(way, c, p, source, pair_flow.at[way, c, p, pl.ds(0, 5 - p)])
+                else:
+                    pair_give(way, c, 4, source.at[0 if way else 1], pair_far.at[way, c], 2, 4)
+                    pair_give(way, c, 3, source.at[1 if way else 0], pair_flow.at[way, c, 3, 0])
+        if p == 1:
+            finish_one()
+    for c in range(PIECES):
+        for way in range(2):
+            pair_wait(way, c, 3)
+            pair_wait(way, c, 4)
+
+    for c in range(PIECES):
+        for r in range(-4, 4):
+            terms = []
+            if -3 <= r <= 0:
+                terms.append(part_pair[c, -r, 0])
+            for p in range(4):
+                if (r + 1 + p) % 8 == 0:
+                    terms.append(pair_flow[0, c, p, 0])
+                if (r + 2 - p) % 8 == 0:
+                    terms.append(pair_flow[1, c, p, 4 - p if p < 3 else 0])
+            if r == 3:
+                terms.append(pair_far[0, c])
+            if r == 2:
+                terms.append(pair_far[1, c])
+            total = jnp.broadcast_to(bias, (16, 512))
+            for term in terms:
+                total += term.astype(jnp.float32)
+            low = pl.multiple_of(ONE + rem(owner + 8 + r, 8) * SUB + c * 16, 16)
+            out_ref[pl.ds(low, 16), :] = total.astype(jnp.bfloat16)
 
     pltpu.make_async_copy(send.at[pl.ds(0, 496), :], send.at[pl.ds(0, 496), :], a2a_send).wait()
     for copy in [scale_copy, z_copy] + sent[0] + sent[1] + pair_copies:
@@ -460,9 +456,9 @@
             pltpu.VMEM((8, ONE, 512), jnp.bfloat16),
             pltpu.VMEM((7, HALF, 512), jnp.bfloat16),
             pltpu.VMEM((7, HALF, 512), jnp.bfloat16),
-            pltpu.VMEM((4, 8, SUB, 512), jnp.bfloat16),
-            pltpu.VMEM((5, 5, SUB, 512), jnp.bfloat16),
-            pltpu.VMEM((5, 5, SUB, 512), jnp.bfloat16),
+            pltpu.VMEM((PIECES, 4, 8, 16, 512), jnp.bfloat16),
+            pltpu.VMEM((2, PIECES, 4, 5, 16, 512), jnp.bfloat16),
+            pltpu.VMEM((2, PIECES, 16, 512), jnp.bfloat16),
             pltpu.VMEM((1, 1024), jnp.float32),
             pltpu.SemaphoreType.DMA((5,)),
             pltpu.SemaphoreType.DMA,
@@ -472,11 +468,10 @@
             pltpu.SemaphoreType.DMA((2,)),
             pltpu.SemaphoreType.DMA((2, 40)),
             pltpu.SemaphoreType.DMA((2, 32)),
-            pltpu.SemaphoreType.DMA((2, 32)),
             pltpu.SemaphoreType.DMA((2, 7)),
             pltpu.SemaphoreType.DMA((2, 7)),
-            pltpu.SemaphoreType.DMA((2, 5)),
-            pltpu.SemaphoreType.DMA((2, 5)),
+            pltpu.SemaphoreType.DMA((2, PIECES, 5)),
+            pltpu.SemaphoreType.DMA((2, PIECES, 5)),
         ],
         compiler_params=pltpu.CompilerParams(
             collective_id=0, has_side_effects=True, vmem_limit_bytes=56 * 1024 * 1024

time: 116 us -> 114 us (0.983)
    pallas_call x1, Pallas kernels: 113 us -> 112 us  [on_device(): call(sample_rows.reshape(8, 128), buffer, window, enc_scale.reshape(1, 10...]
where the time goes in v3:
time: 114 us
  Pallas kernels  112 us (98%)
  local copies, waits for them, and re-layouts  2.06 us (2%)
    pallas_call x1, Pallas kernels, on_device(): call(sample_rows.reshape(8, 128), buffer, window, enc_scale.reshape(1, 10...  112 us

profile of v3, /device:TPU:2, one launch (start us, length us, event | category | flops | bytes accessed | tf_op | source)
XLA Modules:
  0.0 113.7 jit_solution(3666395184422639391)
XLA Ops:
  0.0 111.6 %shard_map.55 = bf16[768,512]{1,0:T(8,128)(2,1)} custom-call(s32[8,128]{1,0:T(8,128)} %bitcast.4, bf16[256,4096]{1,0:T(8,128)(2,1)} %buf_hbm.1, bf16[768,4096]{1,0:T(8,128)(2,1)} %win_hbm.1, f32[1,1024]{1,0:T(1,128)} %bitcast.5, f32[1,4096]{1,0:T(1,128)} %bitcast.3), custom_call_target="tpu_custom_call" | custom-call | tf_op jit(solution)/shard_map/pallas_call | solution.py:480
  111.6 2.1 %copy.7 = bf16[768,512]{1,0:T(8,128)(2,1)} copy(bf16[768,512]{1,0:T(8,128)(2,1)} %shard_map.55) | data formatting | bytes 1572864

commit v4 on v3

--- a/solution.py
+++ b/solution.py
@@ -21,7 +21,7 @@
     rows_ref, buf_hbm, win_hbm, scale_ref, bias_ref, out_ref,
     buf, stage, send, recv, picked, units, cen, cen_pair, act, act_pair,
     part, flow_r, flow_l, part_pair, pair_flow, pair_far, scale_pair,
-    in_sem, own_sem, a2a_send, a2a_recv, z_send, z_recv, ag_send, ag_recv,
+    in_sem, own_sem, a2a_send, a2a_recv, z_send, z_recv, ag_send, ag_recv, ag_recv2,
     rs_send, rs_recv, pair_send, pair_recv,
 ):
     me = lax.axis_index("buf")
@@ -88,7 +88,7 @@
         dc = rem(device, 2)
         dchip = device // 2
         dx, dy = dchip // 4, rem(dchip, 4)
-        return dc * 16 + (dx + dc * (dy - dx)) * 4 + dy + dc * (dx - dy)
+        return dc * 16 + (dy + dc * (dx - dy)) * 4 + dx + dc * (dy - dx)
 
     def tile16(ref, index):
         return ref.at[pl.ds(pl.multiple_of(index * 16, 16), 16), :]
@@ -111,7 +111,7 @@
         return carry
 
     lax.fori_loop(1, 32, push, 0)
-    my_block = core * 16 + a * 4 + b
+    my_block = core * 16 + b * 4 + a
     own_copy = pltpu.make_async_copy(tile16(send, place(my_block)), tile16(recv, me), own_sem)
     own_copy.start()
     scale_copy = pltpu.make_async_remote_copy(
@@ -164,7 +164,7 @@
         units[0, mine_at, q * 512:q * 512 + 512] = (value * inverse).astype(jnp.bfloat16)
 
     def block_at(da, db):
-        return core * 16 + rem(a + da + 4, 4) * 4 + rem(b + db + 4, 4)
+        return core * 16 + rem(b + db + 4, 4) * 4 + rem(a + da + 4, 4)
 
     def device_at(da, db):
         pa, pb = rem(a + da + 4, 4), rem(b + db + 4, 4)
@@ -174,44 +174,71 @@
     sibling = me + 1 - 2 * core
     sent = [[], []]
 
-    mate = 1 - 2 * rem(a, 2)
-
-    def block_ref(w, block):
-        return units.at[w, pl.ds(pl.multiple_of(block * 32, 32), 32), :]
-
-    def give(w, block, target):
-        at = block_ref(w, block)
+    def block_ref(w, block, count=32, half=0):
+        return units.at[w, pl.ds(pl.multiple_of(block * 32 + half * 16, 16), count), :]
+
+    def give(w, block, target, count=32, half=0):
+        at = block_ref(w, block, count, half)
+        sem = ag_recv2 if half else ag_recv
         copy = pltpu.make_async_remote_copy(
             src_ref=at, dst_ref=at, send_sem=ag_send.at[w, len(sent[w])],
-            recv_sem=ag_recv.at[w, block], device_id={"buf": target}, device_id_type=MESH,
+            recv_sem=sem.at[w, block], device_id={"buf": target}, device_id_type=MESH,
         )
         copy.start()
         sent[w].append(copy)
 
-    def arrive(w, block):
-        at = block_ref(w, block)
-        pltpu.make_async_copy(at, at, ag_recv.at[w, block]).wait()
+    def arrive(w, block, count=32, half=0):
+        at = block_ref(w, block, count, half)
+        sem = ag_recv2 if half else ag_recv
+        pltpu.make_async_copy(at, at, sem.at[w, block]).wait()
 
     def spread(w, block):
-        for db in (2, 1, -1):
-            give(w, block, device_at(0, db))
+        give(w, block, device_at(0, 1))
+        give(w, block, device_at(0, -1))
         give(w, block, sibling)
 
+    def second(w, da):
+        block = block_at(da, -1)
+        arrive(w, block)
+        give(w, block, device_at(0, 1), 16, 0)
+        give(w, block, sibling)
+        block = block_at(da, 1)
+        arrive(w, block)
+        give(w, block, device_at(0, -1), 16, 1)
+        give(w, block, sibling)
+
+    def far(w, da):
+        block = block_at(da, 2)
+        arrive(w, block, 16, 0)
+        arrive(w, block, 16, 1)
+        give(w, block, sibling)
+
     def step(w, n):
-        da = (0, mate, -mate, 2)[n % 4]
         if n == 0:
-            for da in (mate, 2, -mate):
-                give(w, my_block, device_at(da, 0))
+            give(w, my_block, device_at(1, 0))
+            give(w, my_block, device_at(-1, 0))
             spread(w, my_block)
-        elif n < 4:
-            block = block_at(da, 0)
+        elif n == 1:
+            block = block_at(-1, 0)
             arrive(w, block)
+            give(w, block, device_at(1, 0), 16, 0)
             spread(w, block)
+        elif n == 2:
+            block = block_at(1, 0)
+            arrive(w, block)
+            give(w, block, device_at(-1, 0), 16, 1)
+            spread(w, block)
+        elif n == 3:
+            second(w, 0)
+        elif n == 4:
+            block = block_at(2, 0)
+            arrive(w, block, 16, 0)
+            arrive(w, block, 16, 1)
+            spread(w, block)
+        elif n < 8:
+            second(w, (-1, 1, 2)[n - 5])
         else:
-            for db in (1, -1, 2):
-                block = block_at(da, db)
-                arrive(w, block)
-                give(w, block, sibling)
+            far(w, (0, -1, 1, 2)[n - 8])
 
     step(0, 0)
     z_copy = pltpu.make_async_remote_copy(
@@ -220,7 +247,7 @@
         device_id={"lat": opposite}, device_id_type=MESH,
     )
     z_copy.start()
-    for n in range(1, 6):
+    for n in range(1, 8):
         step(0, n)
 
     def encode(group):
@@ -239,11 +266,11 @@
         act_pair[w, :, at] = jnp.maximum(scores * scale, 0.0).astype(jnp.bfloat16)
 
     other = 1 - core
-    other_a = y + core * (x - y)
-    mine_near = core * 2 + a // 2
-    mine_far = core * 2 + 1 - a // 2
-    other_near = other * 2 + other_a // 2
-    other_far = other * 2 + 1 - other_a // 2
+    other_b = x + core * (y - x)
+    mine_near = core * 2 + b // 2
+    mine_far = core * 2 + 1 - b // 2
+    other_near = other * 2 + other_b // 2
+    other_far = other * 2 + 1 - other_b // 2
 
     def arrive_group(w, group):
         def one(i, carry):
@@ -253,12 +280,12 @@
         lax.fori_loop(0, 8, one, 0)
 
     encode(mine_near)
-    step(0, 6)
+    for n in range(8, 12):
+        step(0, n)
+    z_copy.wait_recv()
+    step(1, 0)
     arrive_group(0, other_near)
     encode(other_near)
-    step(0, 7)
-    z_copy.wait_recv()
-    step(1, 0)
     encode(mine_far)
     arrive_group(0, other_far)
     encode(other_far)
@@ -303,27 +330,30 @@
     lax.fori_loop(0, 2, decode_next, 0)
     rs_copy(1, half_of(part.at[rem(owner + 3, 8)], 1), flow_r, 0).start()
     rs_copy(1, half_of(part.at[rem(owner + 5, 8)], 0), flow_l, 1).start()
-    for n in range(1, 4):
-        step(1, n)
+    step(1, 1)
+    step(1, 2)
 
     def decode_rest(i, carry):
         decode(rem(owner + 6 + i, 8))
         return carry
 
     lax.fori_loop(0, 5, decode_rest, 0)
+    step(1, 3)
+    hop(2)
     step(1, 4)
-    hop(2)
     lax.fori_loop(0, 4, lambda i, carry: (encode_pair(0, i), carry)[1], 0)
     step(1, 5)
     hop(3)
+    step(1, 6)
     scale_copy.wait_recv()
+    hop(4)
+    step(1, 7)
     encode_pair(1, mine_near)
-    hop(4)
-    step(1, 6)
+    hop(5)
+    for n in range(8, 12):
+        step(1, n)
     arrive_group(1, other_near)
     encode_pair(1, other_near)
-    hop(5)
-    step(1, 7)
     encode_pair(1, mine_far)
     arrive_group(1, other_far)
     encode_pair(1, other_far)
@@ -468,6 +498,7 @@
             pltpu.SemaphoreType.DMA((2,)),
             pltpu.SemaphoreType.DMA((2, 40)),
             pltpu.SemaphoreType.DMA((2, 32)),
+            pltpu.SemaphoreType.DMA((2, 32)),
             pltpu.SemaphoreType.DMA((2, 7)),
             pltpu.SemaphoreType.DMA((2, 7)),
             pltpu.SemaphoreType.DMA((2, PIECES, 5)),

time: 114 us -> 105 us (0.921)
  Pallas kernels: 112 us -> 103 us
    pallas_call x1, Pallas kernels: 112 us -> 103 us  [on_device(): call(sample_rows.reshape(8, 128), buffer, window, enc_scale.reshape(1, 10...]
where the time goes in v4:
time: 105 us
  Pallas kernels  103 us (98%)
  local copies, waits for them, and re-layouts  2.06 us (2%)
    pallas_call x1, Pallas kernels, on_device(): call(sample_rows.reshape(8, 128), buffer, window, enc_scale.reshape(1, 10...  103 us

profile of v4, /device:TPU:2, one launch (start us, length us, event | category | flops | bytes accessed | tf_op | source)
XLA Modules:
  0.0 104.7 jit_solution(9984067708585612919)
XLA Ops:
  0.0 102.6 %shard_map.55 = bf16[768,512]{1,0:T(8,128)(2,1)} custom-call(s32[8,128]{1,0:T(8,128)} %bitcast.4, bf16[256,4096]{1,0:T(8,128)(2,1)} %buf_hbm.1, bf16[768,4096]{1,0:T(8,128)(2,1)} %win_hbm.1, f32[1,1024]{1,0:T(1,128)} %bitcast.5, f32[1,4096]{1,0:T(1,128)} %bitcast.3), custom_call_target="tpu_custom_call" | custom-call | tf_op jit(solution)/shard_map/pallas_call | solution.py:511
  102.6 2.1 %copy.7 = bf16[768,512]{1,0:T(8,128)(2,1)} copy(bf16[768,512]{1,0:T(8,128)(2,1)} %shard_map.55) | data formatting | bytes 1572864

commit v5 on v4

--- a/solution.py
+++ b/solution.py
@@ -18,8 +18,8 @@
 
 
 def fused(
-    rows_ref, buf_hbm, win_hbm, scale_ref, bias_ref, out_ref,
-    buf, stage, send, recv, picked, units, cen, cen_pair, act, act_pair,
+    rows_ref, buf_hbm, win_hbm, scale_ref, bias_ref, out_hbm,
+    out_ref,    buf, stage, send, recv, picked, units, cen, cen_pair, act, act_pair,
     part, flow_r, flow_l, part_pair, pair_flow, pair_far, scale_pair,
     in_sem, own_sem, a2a_send, a2a_recv, z_send, z_recv, ag_send, ag_recv, ag_recv2,
     rs_send, rs_recv, pair_send, pair_recv,
@@ -280,12 +280,12 @@
         lax.fori_loop(0, 8, one, 0)
 
     encode(mine_near)
+    arrive_group(0, other_near)
+    encode(other_near)
     for n in range(8, 12):
         step(0, n)
     z_copy.wait_recv()
     step(1, 0)
-    arrive_group(0, other_near)
-    encode(other_near)
     encode(mine_far)
     arrive_group(0, other_far)
     encode(other_far)
@@ -399,6 +399,10 @@
 
     bias = bias_ref[:, pl.ds(pl.multiple_of(owner * 512, 512), 512)]
 
+    def out_copy(n):
+        at = pl.ds(ONE, 768 - ONE) if n else pl.ds(0, ONE)
+        return pltpu.make_async_copy(out_ref.at[at, :], out_hbm.at[at, :], in_sem.at[n])
+
     def finish_one():
         for i in (5, 6):
             rs_wait(i, flow_r, 0)
@@ -408,6 +412,7 @@
             total = part[owner, at, :].astype(jnp.float32) + bias
             total += flow_r[6 - half].astype(jnp.float32) + flow_l[5 + half].astype(jnp.float32)
             out_ref[at, :] = total.astype(jnp.bfloat16)
+        out_copy(0).start()
 
     for p in range(1, 4):
         for c in range(PIECES):
@@ -452,6 +457,8 @@
             low = pl.multiple_of(ONE + rem(owner + 8 + r, 8) * SUB + c * 16, 16)
             out_ref[pl.ds(low, 16), :] = total.astype(jnp.bfloat16)
 
+    out_copy(1).start()
+
     pltpu.make_async_copy(send.at[pl.ds(0, 496), :], send.at[pl.ds(0, 496), :], a2a_send).wait()
     for copy in [scale_copy, z_copy] + sent[0] + sent[1] + pair_copies:
         copy.wait_send()
@@ -462,6 +469,8 @@
         return carry
 
     lax.fori_loop(0, 7, drain, 0)
+    out_copy(0).wait()
+    out_copy(1).wait()
 
 
 def on_device(buffer, sample_rows, window, enc_scale, dec_bias):
@@ -471,8 +480,9 @@
         fused,
         out_shape=jax.ShapeDtypeStruct((768, 512), jnp.bfloat16),
         in_specs=[vmem, anywhere, anywhere, vmem, vmem],
-        out_specs=vmem,
+        out_specs=anywhere,
         scratch_shapes=[
+            pltpu.VMEM((768, 512), jnp.bfloat16),
             pltpu.VMEM((256, 4096), jnp.bfloat16),
             pltpu.VMEM((4, 512, 128), jnp.float32),
             pltpu.VMEM((512, 512), jnp.bfloat16),
@@ -505,7 +515,7 @@
             pltpu.SemaphoreType.DMA((2, PIECES, 5)),
         ],
         compiler_params=pltpu.CompilerParams(
-            collective_id=0, has_side_effects=True, vmem_limit_bytes=56 * 1024 * 1024
+            collective_id=0, has_side_effects=True, vmem_limit_bytes=52 * 1024 * 1024
         ),
     )
     return call(

time: 105 us -> 104 us (level)
  Pallas kernels: 103 us -> 101 us
    pallas_call x1, Pallas kernels: 103 us -> 101 us  [on_device(): call(sample_rows.reshape(8, 128), buffer, window, enc_scale.reshape(1, 10...]
    unnamed x1 -> x7, local copies, waits for them, and re-layouts: 2.06 us -> 2.97 us
where the time goes in v5:
time: 104 us
  Pallas kernels  101 us (97%)
  local copies, waits for them, and re-layouts  2.97 us (3%)
    pallas_call x1, Pallas kernels, on_device(): call(sample_rows.reshape(8, 128), buffer, window, enc_scale.reshape(1, 10...  101 us
    unnamed x7, local copies, waits for them, and re-layouts  2.97 us

profile of v5, /device:TPU:2, one launch (start us, length us, event | category | flops | bytes accessed | tf_op | source)
XLA Modules:
  0.0 104.2 jit_solution(10461229015637107428)
XLA Ops:
  0.0 0.0 copy-start
  0.0 0.7 copy-done
  0.7 0.0 copy-start.1
  0.7 0.7 copy-done.1
  1.4 0.0 copy-start.2
  1.4 0.7 copy-done.2
  2.1 101.2 %shard_map.55 = bf16[768,512]{1,0:T(8,128)(2,1)S(1)} custom-call(s32[8,128]{1,0:T(8,128)S(1)} %bitcast.4, bf16[256,4096]{1,0:T(8,128)(2,1)} %buf_hbm.1, bf16[768,4096]{1,0:T(8,128)(2,1)} %win_hbm.1, f32[1,1024]{1,0:T(1,128)S(1)} %bitcast.5, f32[1,4096]{1,0:T(1,128)S(1)} %bitcast.3), custom_call_target="tpu_custom_call" | custom-call | tf_op jit(solution)/shard_map/pallas_call | solution.py:521
  103.3 0.9 copy.7
Async XLA Ops:
  0.0 0.7 copy-start
  0.7 0.7 copy-start.1
  1.4 0.7 copy-start.2

commit v6 on v5

--- a/solution.py
+++ b/solution.py
@@ -319,9 +319,14 @@
             flow[i - 2] = total.astype(jnp.bfloat16)
             rs_copy(i, flow.at[i - 2], flow, way).start()
 
-    decode(opposite)
-    rs_copy(0, half_of(part.at[opposite], 0), flow_r, 0).start()
-    rs_copy(0, half_of(part.at[opposite], 1), flow_l, 1).start()
+    for way, flow in ((0, flow_r), (1, flow_l)):
+        columns = pl.ds(pl.multiple_of(opposite * 512, 512), 512)
+        rows_at = slice(way * HALF, way * HALF + HALF)
+        value = jnp.dot(
+            act[rows_at, :], units[0, :, columns], preferred_element_type=jnp.float32
+        )
+        part[opposite, rows_at, :] = value.astype(jnp.bfloat16)
+        rs_copy(0, half_of(part.at[opposite], way), flow, way).start()
 
     def decode_next(i, carry):
         decode(rem(owner + 3 + 2 * i, 8))
@@ -339,10 +344,10 @@
 
     lax.fori_loop(0, 5, decode_rest, 0)
     step(1, 3)
+    step(1, 4)
     hop(2)
-    step(1, 4)
+    step(1, 5)
     lax.fori_loop(0, 4, lambda i, carry: (encode_pair(0, i), carry)[1], 0)
-    step(1, 5)
     hop(3)
     step(1, 6)
     scale_copy.wait_recv()

time: 104 us -> 105 us (level)
  no operation moved by 1% of the time
where the time goes in v6:
time: 105 us
  Pallas kernels  102 us (97%)
  local copies, waits for them, and re-layouts  2.97 us (3%)
    pallas_call x1, Pallas kernels, on_device(): call(sample_rows.reshape(8, 128), buffer, window, enc_scale.reshape(1, 10...  102 us
    unnamed x7, local copies, waits for them, and re-layouts  2.97 us

profile of v6, /device:TPU:2, one launch (start us, length us, event | category | flops | bytes accessed | tf_op | source)
XLA Modules:
  0.0 104.5 jit_solution(12251959124226948328)
XLA Ops:
  0.0 0.0 copy-start
  0.0 0.7 copy-done
  0.7 0.0 copy-start.1
  0.7 0.7 copy-done.1
  1.4 0.0 copy-start.2
  1.4 0.7 copy-done.2
  2.1 101.6 %shard_map.55 = bf16[768,512]{1,0:T(8,128)(2,1)S(1)} custom-call(s32[8,128]{1,0:T(8,128)S(1)} %bitcast.4, bf16[256,4096]{1,0:T(8,128)(2,1)} %buf_hbm.1, bf16[768,4096]{1,0:T(8,128)(2,1)} %win_hbm.1, f32[1,1024]{1,0:T(1,128)S(1)} %bitcast.5, f32[1,4096]{1,0:T(1,128)S(1)} %bitcast.3), custom_call_target="tpu_custom_call" | custom-call | tf_op jit(solution)/shard_map/pallas_call | solution.py:526
  103.7 0.9 copy.7
Async XLA Ops:
  0.0 0.7 copy-start
  0.7 0.7 copy-start.1
  1.4 0.7 copy-start.2
